TPU v7x, 256 devices: a whole 4x4x8 slice. The times are simulated.
256 devices in a mesh: dp: 8 (over x, core), tm: 32 (over z, y).
Axes of the slice: x: 4, y: 4, z: 8, core: 2. Of those that a mesh axis runs over, the one named last changes fastest.
Arguments:
- latents: bfloat16 [8, 17, 64, 64, 256], P('dp', None, 'tm'), may hold values from -6 to 6
- cotangent: bfloat16 [8, 17, 64, 64, 256], P('dp', None, 'tm'), may hold values from -6 to 6
- spatial_weight: bfloat16 [3, 3, 256, 256], replicated, may hold values from -0.125 to 0.125
- temporal_weight: bfloat16 [3, 256, 256], replicated, may hold values from -0.21875 to 0.21875
Outputs:
- block_out: bfloat16 [8, 17, 64, 64, 256], P('dp', None, 'tm')
- latents_grad: bfloat16 [8, 17, 64, 64, 256], P('dp', None, 'tm')
- spatial_grad: float32 [3, 3, 256, 256], replicated
- temporal_grad: float32 [3, 256, 256], replicated
All inputs are finite; a program needn't handle non-finite values.
Results may differ from a plain program's by a relative error of at most 0.0085.
Values may be sent and summed in bfloat16 or wider, within the bound.
A program may use at most 64 MiB of HBM per device.

v0:
```python
import jax
import jax.numpy as jnp
from jax import lax
from jax.sharding import PartitionSpec as P


def with_halo(cells, sides, width):
    for axis, dim in sides:
        count = lax.axis_size(axis)
        ends = count - 1
        head = lax.slice_in_dim(cells, 0, width, axis=dim)
        tail = lax.slice_in_dim(cells, cells.shape[dim] - width, cells.shape[dim], axis=dim)
        cells = jnp.concatenate(
            [
                lax.ppermute(tail, axis, [(i, (i + 1) % count) for i in range(ends)]),
                cells,
                lax.ppermute(head, axis, [((i + 1) % count, i) for i in range(ends)]),
            ],
            axis=dim,
        )
    return cells


def band_patches(extended, rows_out, flipped):
    padded = jnp.pad(extended, ((0, 0), (0, 0), (1, 1), (0, 0)))
    cols = extended.shape[2]
    pieces = []
    for first in range(3):
        for second in range(3):
            top = 2 - first if flipped else first
            left = 2 - second if flipped else second
            pieces.append(padded[:, top : top + rows_out, left : left + cols, :])
    return jnp.concatenate(pieces, axis=3).reshape(-1, 9 * extended.shape[3])


def causal_mix(act, weight):
    clips, frames, cells, chans = act.shape
    padded = jnp.pad(act, ((0, 0), (2, 0), (0, 0), (0, 0)))
    total = jnp.zeros((clips * frames * cells, chans), jnp.float32)
    for tap in range(3):
        earlier = padded[:, 2 - tap : 2 - tap + frames].reshape(-1, chans)
        total = total + jnp.dot(earlier, weight[tap], preferred_element_type=jnp.float32)
    return total.astype(jnp.bfloat16)


def anti_mix(cot, weight):
    clips, frames, cells, chans = cot.shape
    padded = jnp.pad(cot, ((0, 0), (0, 2), (0, 0), (0, 0)))
    total = jnp.zeros((clips * frames * cells, chans), jnp.float32)
    for tap in range(3):
        later = padded[:, tap : tap + frames].reshape(-1, chans)
        total = total + lax.dot_general(
            later, weight[tap], (((1,), (1,)), ((), ())), preferred_element_type=jnp.float32
        )
    return total.astype(jnp.bfloat16)


def tap_grads(act, cot):
    clips, frames, cells, chans = act.shape
    padded = jnp.pad(act, ((0, 0), (2, 0), (0, 0), (0, 0)))
    cot_flat = cot.reshape(-1, chans)
    parts = []
    for tap in range(3):
        earlier = padded[:, 2 - tap : 2 - tap + frames].reshape(-1, chans)
        parts.append(
            lax.dot_general(
                earlier, cot_flat, (((0,), (0,)), ((), ())), preferred_element_type=jnp.float32
            )
        )
    return jnp.stack(parts)


def silu_grad(act_grad, pre):
    sig = jax.nn.sigmoid(pre)
    return (act_grad.astype(jnp.float32) * sig * (1.0 + pre * (1.0 - sig))).astype(jnp.bfloat16)


def body(latents, cotangent, spatial_weight, temporal_weight):
    clips, frames, rows, cols, chans = latents.shape
    flat_w = spatial_weight.reshape(9 * chans, chans)
    flip_w = jnp.transpose(spatial_weight, (0, 1, 3, 2)).reshape(9 * chans, chans)
    cot_band = cotangent.reshape(clips, frames, rows * cols, chans)
    extended = with_halo(latents, (("tm", 2),), 1)
    patches = band_patches(extended.reshape(clips * frames, rows + 2, cols, chans), rows, False)
    pre = jnp.dot(patches, flat_w, preferred_element_type=jnp.float32)
    act = jax.nn.silu(pre).astype(jnp.bfloat16).reshape(clips, frames, rows * cols, chans)
    mixed = causal_mix(act, temporal_weight)
    act_grad = anti_mix(cot_band, temporal_weight)
    pre_grad = silu_grad(act_grad, pre)
    grad_ext = with_halo(pre_grad.reshape(clips, frames, rows, cols, chans), (("tm", 2),), 1)
    back = jnp.dot(
        band_patches(grad_ext.reshape(clips * frames, rows + 2, cols, chans), rows, True),
        flip_w,
        preferred_element_type=jnp.float32,
    )
    temporal_local = tap_grads(act, cot_band)
    block_out = (latents.reshape(-1, chans).astype(jnp.float32) + mixed.astype(jnp.float32)).astype(
        jnp.bfloat16
    )
    latents_grad = (cotangent.reshape(-1, chans).astype(jnp.float32) + back).astype(jnp.bfloat16)
    spatial_local = lax.dot_general(
        patches, pre_grad, (((0,), (0,)), ((), ())), preferred_element_type=jnp.float32
    )
    spatial_sum, temporal_sum = lax.psum((spatial_local, temporal_local), ("dp", "tm"))
    scale = (clips * lax.axis_size("dp") * frames * rows * lax.axis_size("tm") * cols) ** (-0.5)
    return (
        block_out.reshape(latents.shape),
        latents_grad.reshape(latents.shape),
        (spatial_sum * scale).reshape(3, 3, chans, chans),
        temporal_sum * scale,
    )


def solution(mesh):
    in_specs = (P("dp", None, "tm", None, None), P("dp", None, "tm", None, None), P(), P())
    out_specs = (P("dp", None, "tm", None, None), P("dp", None, "tm", None, None), P(), P())
    return jax.shard_map(body, mesh=mesh, in_specs=in_specs, out_specs=out_specs, check_vma=False)
```

profile of v0, /device:TPU:2, one launch (start us, length us, event | category | flops | bytes accessed | tf_op | source)
XLA Modules:
  0.0 338.0 jit_solution(11071545228273672446)
XLA Ops:
  7.2 2.4 fusion.37
  9.6 4.4 %collective-permute-start = (bf16[1,17,1,64,256]{4,3,2,1,0:T(8,128)(2,1)}, bf16[1,17,1,64,256]{4,3,2,1,0:T(8,128)(2,1)}, u32[]{:S(2)}, u32[]{:S(2)}) collective-permute-start(bf16[1,17,1,64,256]{4,3,2,1,0:T(8,128)(2,1)} %get-tuple-element.12), channel_id=1, source_target_pairs={{0,1},{1,2},{2,3},{3,4},{4,5},{5,6},{6,7},{7,8},{8,9},{9,10},{10,1... | collective-permute-start | bytes 1671176 | tf_op jit(solution)/shard_map/ppermute | solution.py:15
  14.1 1.3 collective-permute-start.1
  15.4 2.8 fusion.26
  18.1 1.5 copy.8
  19.7 0.2 pad_slice_fusion.12
  19.9 1.4 copy-done.3
  21.3 0.5 convolution_add_fusion.1
  21.8 3.6 %collective-permute-done = bf16[1,17,1,64,256]{4,3,2,1,0:T(8,128)(2,1)} collective-permute-done((bf16[1,17,1,64,256]{4,3,2,1,0:T(8,128)(2,1)}, bf16[1,17,1,64,256]{4,3,2,1,0:T(8,128)(2,1)}, u32[]{:S(2)}, u32[]{:S(2)}) %collective-permute-start) | collective-permute-done | bytes 557088 | tf_op jit(solution)/shard_map/ppermute | solution.py:15
  25.4 4.9 %collective-permute-done.1 = bf16[1,17,1,64,256]{4,3,2,1,0:T(8,128)(2,1)} collective-permute-done((bf16[1,17,1,64,256]{4,3,2,1,0:T(8,128)(2,1)}, bf16[1,17,1,64,256]{4,3,2,1,0:T(8,128)(2,1)}, u32[]{:S(2)}, u32[]{:S(2)}) %collective-permute-start.1) | collective-permute-done | bytes 557088 | tf_op jit(solution)/shard_map/ppermute | solution.py:17
  30.4 1.5 maximum_bitcast_fusion
  31.8 0.4 fusion.10
  32.2 0.1 slice_dynamic-update-slice_fusion.5
  32.3 0.6 fusion.11
  32.9 0.7 fusion.12
  33.7 0.6 fusion.13
  34.3 0.7 fusion.14
  35.0 0.1 slice_dynamic-update-slice_fusion.3
  35.1 0.6 fusion.15
  35.7 2.9 multiply_convert_fusion
  38.6 0.5 convolution_bitcast_fusion.2
  39.1 1.8 fusion.28
  41.0 1.0 fusion.9
  42.0 4.4 %fusion.38 = f32[2304,256]{1,0:T(8,128)} fusion(bf16[2176,2304]{1,0:T(8,128)(2,1)S(1)} %bitcast.83, bf16[2176,256]{1,0:T(8,128)(2,1)S(1)} %fusion.9), kind=kOutput, calls=%fused_computation.75 | convolution fusion | flops 2566914048 | bytes 13500416 | tf_op jit(solution)/shard_map/dot_general | solution.py:101
  46.4 1.2 fusion.36
  47.6 3.5 %collective-permute-start.2 = (bf16[1,17,1,64,256]{4,3,2,1,0:T(8,128)(2,1)}, bf16[1,17,1,64,256]{4,3,2,1,0:T(8,128)(2,1)}, u32[]{:S(2)}, u32[]{:S(2)}) collective-permute-start(bf16[1,17,1,64,256]{4,3,2,1,0:T(8,128)(2,1)} %get-tuple-element.6), channel_id=1, source_target_pairs={{0,1},{1,2},{2,3},{3,4},{4,5},{5,6},{6,7},{7,8},{8,9},{9,10},{10,1... | collective-permute-start | bytes 1671176 | tf_op jit(solution)/shard_map/ppermute | solution.py:15
  51.2 1.3 collective-permute-start.3
  52.4 0.1 pad_slice_fusion.14
  52.6 0.5 convolution_bitcast_fusion
  53.1 0.5 convolution_bitcast_fusion.1
  53.6 0.9 pad_maximum_fusion
  54.6 2.5 convolution_add_fusion.3
  57.1 2.5 fusion.4
  59.6 1.8 collective-permute-done.2
  61.4 4.9 %collective-permute-done.3 = bf16[1,17,1,64,256]{4,3,2,1,0:T(8,128)(2,1)} collective-permute-done((bf16[1,17,1,64,256]{4,3,2,1,0:T(8,128)(2,1)}, bf16[1,17,1,64,256]{4,3,2,1,0:T(8,128)(2,1)}, u32[]{:S(2)}, u32[]{:S(2)}) %collective-permute-start.3) | collective-permute-done | bytes 557088 | tf_op jit(solution)/shard_map/ppermute | solution.py:17
  66.3 1.5 maximum_bitcast_fusion.1
  67.8 0.3 fusion.16
  68.1 0.1 slice_dynamic-update-slice_fusion.2
  68.3 0.7 fusion.17
  69.0 0.6 fusion.18
  69.7 0.7 fusion.19
  70.4 0.6 fusion.20
  71.1 0.7 fusion.21
  71.8 0.6 copy-done.7
  72.3 3.8 %fusion = bf16[2176,256]{1,0:T(8,128)(2,1)} fusion(bf16[2176,2304]{1,0:T(8,128)(2,1)S(1)} %bitcast.84, bf16[2304,256]{1,0:T(8,128)(2,1)S(1)} %bitcast.79, bf16[2176,256]{1,0:T(8,128)(2,1)S(1)} %bitcast.67), kind=kOutput, calls=%fused_computation.5 | convolution fusion | flops 2568585216 | bytes 13434880 | tf_op jit(solution)/shard_map/dot_general | solution.py:91
  76.1 250.7 %all-reduce.7.cloned.1.call-done = (f32[2304,256]{1,0:T(8,128)}, f32[3,256,256]{2,1,0:T(8,128)}) async-done(((f32[2304,256]{1,0:T(8,128)}, f32[3,256,256]{2,1,0:T(8,128)}), (f32[2304,256]{1,0:T(8,128)}, f32[3,256,256]{2,1,0:T(8,128)})) %all-reduce.7.cloned.1.call-update) | async-done | bytes 3145744 | tf_op jit(solution)/shard_map/psum | solution.py:104
  326.8 3.3 broadcast_multiply_fusion
  330.2 0.9 broadcast_multiply_fusion.1
  (23 shorter events, 0.4 us)
Async XLA Ops:
  7.2 8.2 %copy-start = (bf16[1,17,2,64,256]{4,3,2,1,0:T(8,128)(2,1)S(1)}, bf16[1,17,2,64,256]{4,3,2,1,0:T(8,128)(2,1)}, u32[]{:S(2)}) copy-start(bf16[1,17,2,64,256]{4,3,2,1,0:T(8,128)(2,1)} %param.5) | copy-start | bytes 3342340
  7.2 319.6 %all-reduce.7.cloned.1.call-start = ((), (), s32[]{:S(2)}) async-start(), calls=%async_computation | async-start | bytes 6291456 | tf_op jit(solution)/shard_map/psum | solution.py:104
  9.6 8.5 %copy-start.6 = (bf16[3,3,256,256]{3,2,1,0:T(8,128)(2,1)S(1)}, bf16[3,3,256,256]{3,2,1,0:T(8,128)(2,1)}, u32[]{:S(2)}) copy-start(bf16[3,3,256,256]{3,2,1,0:T(8,128)(2,1)} %param.6) | copy-start | bytes 3538948
  9.6 15.8 %collective-permute-start = (bf16[1,17,1,64,256]{4,3,2,1,0:T(8,128)(2,1)}, bf16[1,17,1,64,256]{4,3,2,1,0:T(8,128)(2,1)}, u32[]{:S(2)}, u32[]{:S(2)}) collective-permute-start(bf16[1,17,1,64,256]{4,3,2,1,0:T(8,128)(2,1)} %get-tuple-element.12), channel_id=1, source_target_pairs={{0,1},{1,2},{2,3},{3,4},{4,5},{5,6},{6,7},{7,8},{8,9},{9,10},{10,1... | collective-permute-start | bytes 1671176 | tf_op jit(solution)/shard_map/ppermute | solution.py:15
  14.1 16.3 %collective-permute-start.1 = (bf16[1,17,1,64,256]{4,3,2,1,0:T(8,128)(2,1)}, bf16[1,17,1,64,256]{4,3,2,1,0:T(8,128)(2,1)}, u32[]{:S(2)}, u32[]{:S(2)}) collective-permute-start(bf16[1,17,1,64,256]{4,3,2,1,0:T(8,128)(2,1)} %get-tuple-element.13), channel_id=1, source_target_pairs={{1,0},{2,1},{3,2},{4,3},{5,4},{6,5},{7,6},{8,7},{9,8},{10,9},{11,1... | collective-permute-start | bytes 1671176 | tf_op jit(solution)/shard_map/ppermute | solution.py:17
  19.7 1.6 copy-start.3
  19.7 1.7 copy-start.8
  21.3 9.0 %copy-start.1 = (bf16[1,17,2,64,256]{4,3,2,1,0:T(8,128)(2,1)S(1)}, bf16[1,17,2,64,256]{4,3,2,1,0:T(8,128)(2,1)}, u32[]{:S(2)}) copy-start(bf16[1,17,2,64,256]{4,3,2,1,0:T(8,128)(2,1)} %param.4) | copy-start | bytes 3342340
  42.0 4.4 %copy-start.4 = (bf16[2176,256]{1,0:T(8,128)(2,1)}, bf16[2176,256]{1,0:T(8,128)(2,1)S(1)}, u32[]{:S(2)}) copy-start(bf16[2176,256]{1,0:T(8,128)(2,1)S(1)} %fusion.9) | copy-start | bytes 3342340
  47.6 13.7 %collective-permute-start.2 = (bf16[1,17,1,64,256]{4,3,2,1,0:T(8,128)(2,1)}, bf16[1,17,1,64,256]{4,3,2,1,0:T(8,128)(2,1)}, u32[]{:S(2)}, u32[]{:S(2)}) collective-permute-start(bf16[1,17,1,64,256]{4,3,2,1,0:T(8,128)(2,1)} %get-tuple-element.6), channel_id=1, source_target_pairs={{0,1},{1,2},{2,3},{3,4},{4,5},{5,6},{6,7},{7,8},{8,9},{9,10},{10,1... | collective-permute-start | bytes 1671176 | tf_op jit(solution)/shard_map/ppermute | solution.py:15
  51.2 15.1 %collective-permute-start.3 = (bf16[1,17,1,64,256]{4,3,2,1,0:T(8,128)(2,1)}, bf16[1,17,1,64,256]{4,3,2,1,0:T(8,128)(2,1)}, u32[]{:S(2)}, u32[]{:S(2)}) collective-permute-start(bf16[1,17,1,64,256]{4,3,2,1,0:T(8,128)(2,1)} %get-tuple-element.7), channel_id=1, source_target_pairs={{1,0},{2,1},{3,2},{4,3},{5,4},{6,5},{7,6},{8,7},{9,8},{10,9},{11,1... | collective-permute-start | bytes 1671176 | tf_op jit(solution)/shard_map/ppermute | solution.py:17
  52.6 1.0 copy-start.2
  57.1 9.2 %copy-start.5 = (bf16[2176,256]{1,0:T(8,128)(2,1)S(1)}, bf16[2176,256]{1,0:T(8,128)(2,1)}, u32[]{:S(2)}) copy-start(bf16[2176,256]{1,0:T(8,128)(2,1)} %copy-done.4) | copy-start | bytes 3342340
  71.0 1.3 copy-start.7
  326.8 3.4 copy-start.9
Sparse Core Ops, SparseCore 0:
  54.7 272.0 all-reduce.6
where the time goes:
time: 338 us
  waiting for transfers between devices  266 us (79%)
  matrix products  23.6 us (7%)
  local copies, waits for them, and re-layouts  15.4 us (5%)
  between operations  14.3 us (4%)
  starting transfers between devices  10.5 us (3%)
  other arithmetic  8.16 us (2%)
    psum x1, waiting for transfers between devices, body(): lax.psum((spatial_local, temporal_local), ('dp', 'tm'))  251 us
    unnamed x37, local copies, waits for them, and re-layouts  10.1 us
    ppermute x2, waiting for transfers between devices, with_halo(): lax.ppermute(head, axis, [((i + 1) % count, i) for i in range(ends)])  9.86 us
    ppermute x2, starting transfers between devices, with_halo(): lax.ppermute(tail, axis, [(i, (i + 1) % count) for i in range(ends)])  7.93 us
    dot_general x3, matrix products, causal_mix(): jnp.dot(earlier, weight[tap], preferred_element_type=jnp.float32)  6.79 us
  transfers between devices with their start and end apart: 5, of which 5 were waited for; matrix products, arithmetic and copies ran while one was open for 6% of the time, Pallas kernels for 0%

commit v1 on v0

--- a/solution.py
+++ b/solution.py
@@ -2,6 +2,7 @@
 import jax.numpy as jnp
 from jax import lax
 from jax.sharding import PartitionSpec as P
+from jax.lax import psum
 
 
 def with_halo(cells, sides, width):
@@ -101,7 +102,7 @@
     spatial_local = lax.dot_general(
         patches, pre_grad, (((0,), (0,)), ((), ())), preferred_element_type=jnp.float32
     )
-    spatial_sum, temporal_sum = lax.psum((spatial_local, temporal_local), ("dp", "tm"))
+    spatial_sum, temporal_sum = psum(psum((spatial_local, temporal_local), "dp"), "tm")
     scale = (clips * lax.axis_size("dp") * frames * rows * lax.axis_size("tm") * cols) ** (-0.5)
     return (
         block_out.reshape(latents.shape),

time: 338 us -> 297 us (0.88)
  waiting for transfers between devices: 266 us -> 227 us
    psum x1 -> x2, waiting for transfers between devices: 251 us -> 214 us  [the longest x1 150 us: body(): psum(psum((spatial_local, temporal_local), 'dp'), 'tm')]
    ppermute x2, waiting for transfers between devices: 9.86 us -> 4.15 us  [with_halo(): lax.ppermute(head, axis, [((i + 1) % count, i) for i in range(ends)])]
    ppermute x2, waiting for transfers between devices: 5.39 us -> 9.35 us  [with_halo(): lax.ppermute(tail, axis, [(i, (i + 1) % count) for i in range(ends)])]
    unnamed x37 -> x39, local copies, waits for them, and re-layouts: 10.1 us -> 10.1 us
  transfers between devices with their start and end apart: 5 -> 6, of which waited for: 5 -> 4; matrix products, arithmetic and copies ran while one was open for 6% -> 8% of each run, Pallas kernels for 0% -> 0%
where the time goes in v1:
time: 297 us
  waiting for transfers between devices  227 us (76%)
  matrix products  22.3 us (8%)
  local copies, waits for them, and re-layouts  15.8 us (5%)
  between operations  14.4 us (5%)
  starting transfers between devices  10.4 us (4%)
  other arithmetic  6.95 us (2%)
    psum x1, waiting for transfers between devices, body(): psum(psum((spatial_local, temporal_local), 'dp'), 'tm')  150 us
    psum x1, waiting for transfers between devices, body(): psum((spatial_local, temporal_local), 'dp')  63.5 us
    unnamed x39, local copies, waits for them, and re-layouts  10.1 us
    ppermute x2, waiting for transfers between devices, with_halo(): lax.ppermute(tail, axis, [(i, (i + 1) % count) for i in range(ends)])  9.35 us
    ppermute x2, starting transfers between devices, with_halo(): lax.ppermute(tail, axis, [(i, (i + 1) % count) for i in range(ends)])  7.78 us
    dot_general x3, matrix products, causal_mix(): jnp.dot(earlier, weight[tap], preferred_element_type=jnp.float32)  7.72 us
  transfers between devices with their start and end apart: 6, of which 4 were waited for; matrix products, arithmetic and copies ran while one was open for 8% of the time, Pallas kernels for 0%

profile of v1, /device:TPU:2, one launch (start us, length us, event | category | flops | bytes accessed | tf_op | source)
XLA Modules:
  0.0 297.0 jit_solution(10611479128560798154)
XLA Ops:
  7.2 1.4 fusion.37
  8.6 3.5 %collective-permute-start = (bf16[1,17,1,64,256]{4,3,2,1,0:T(8,128)(2,1)S(1)}, bf16[1,17,1,64,256]{4,3,2,1,0:T(8,128)(2,1)S(1)}, u32[]{:S(2)}, u32[]{:S(2)}) collective-permute-start(bf16[1,17,1,64,256]{4,3,2,1,0:T(8,128)(2,1)S(1)} %get-tuple-element.14), channel_id=1, source_target_pairs={{0,1},{1,2},{2,3},{3,4},{4,5},{5,6},{6,7},{7,8},{8,9},{9,10},{10,1... | collective-permute-start | bytes 1671176 | tf_op jit(solution)/shard_map/ppermute | solution.py:16
  12.2 1.3 collective-permute-start.1
  13.5 0.5 fusion.26
  14.0 0.2 pad_slice_fusion.12
  14.2 0.5 convolution_add_fusion.1
  14.7 9.3 %collective-permute-done = bf16[1,17,1,64,256]{4,3,2,1,0:T(8,128)(2,1)S(1)} collective-permute-done((bf16[1,17,1,64,256]{4,3,2,1,0:T(8,128)(2,1)S(1)}, bf16[1,17,1,64,256]{4,3,2,1,0:T(8,128)(2,1)S(1)}, u32[]{:S(2)}, u32[]{:S(2)}) %collective-permute-start) | collective-permute-done | bytes 557088 | tf_op jit(solution)/shard_map/ppermute | solution.py:16
  24.0 4.1 %collective-permute-done.1 = bf16[1,17,1,64,256]{4,3,2,1,0:T(8,128)(2,1)S(1)} collective-permute-done((bf16[1,17,1,64,256]{4,3,2,1,0:T(8,128)(2,1)S(1)}, bf16[1,17,1,64,256]{4,3,2,1,0:T(8,128)(2,1)S(1)}, u32[]{:S(2)}, u32[]{:S(2)}) %collective-permute-start.1) | collective-permute-done | bytes 557088 | tf_op jit(solution)/shard_map/ppermute | solution.py:18
  28.1 0.2 maximum_bitcast_fusion
  28.4 0.4 fusion.10
  28.8 0.1 slice_dynamic-update-slice_fusion.5
  28.8 0.6 fusion.11
  29.4 0.7 fusion.12
  30.1 0.1 slice_dynamic-update-slice_fusion.4
  30.3 0.6 fusion.13
  30.9 0.7 fusion.14
  31.6 0.1 slice_dynamic-update-slice_fusion.3
  31.7 0.6 fusion.15
  32.3 0.7 copy-done.7
  32.9 2.9 multiply_convert_fusion
  35.9 1.0 fusion.9
  36.9 4.4 %fusion.38 = f32[2304,256]{1,0:T(8,128)} fusion(bf16[2176,2304]{1,0:T(8,128)(2,1)S(1)} %bitcast.83, bf16[2176,256]{1,0:T(8,128)(2,1)S(1)} %fusion.9), kind=kOutput, calls=%fused_computation.75 | convolution fusion | flops 2566914048 | bytes 13500416 | tf_op jit(solution)/shard_map/dot_general | solution.py:102
  41.3 0.5 convolution_bitcast_fusion.2
  41.8 0.3 pad_slice_fusion.14
  42.2 0.5 convolution_bitcast_fusion
  42.7 0.5 convolution_bitcast_fusion.1
  43.2 0.9 pad_maximum_fusion
  44.2 2.4 copy.8
  46.6 2.5 fusion.36
  49.1 4.3 %collective-permute-start.2 = (bf16[1,17,1,64,256]{4,3,2,1,0:T(8,128)(2,1)}, bf16[1,17,1,64,256]{4,3,2,1,0:T(8,128)(2,1)}, u32[]{:S(2)}, u32[]{:S(2)}) collective-permute-start(bf16[1,17,1,64,256]{4,3,2,1,0:T(8,128)(2,1)} %get-tuple-element.8), channel_id=1, source_target_pairs={{0,1},{1,2},{2,3},{3,4},{4,5},{5,6},{6,7},{7,8},{8,9},{9,10},{10,1... | collective-permute-start | bytes 1671176 | tf_op jit(solution)/shard_map/ppermute | solution.py:16
  53.4 1.3 collective-permute-start.3
  54.7 2.8 fusion.28
  57.4 63.5 %all-reduce.11.cloned.1.call-done = (f32[2304,256]{1,0:T(8,128)}, f32[3,256,256]{2,1,0:T(8,128)}) async-done(((f32[2304,256]{1,0:T(8,128)}, f32[3,256,256]{2,1,0:T(8,128)}), (f32[2304,256]{1,0:T(8,128)}, f32[3,256,256]{2,1,0:T(8,128)})) %all-reduce.11.cloned.1.call-update) | async-done | bytes 3145744 | tf_op jit(solution)/shard_map/psum | solution.py:105
  120.9 2.5 convolution_add_fusion.3
  123.4 2.5 fusion.4
  125.9 1.5 maximum_bitcast_fusion.1
  127.4 0.3 fusion.16
  127.8 0.1 slice_dynamic-update-slice_fusion.2
  127.9 0.7 fusion.17
  128.6 0.6 fusion.18
  129.3 0.7 fusion.19
  130.0 0.6 fusion.20
  130.7 0.7 fusion.21
  131.4 0.6 copy-done.8
  131.9 3.8 %fusion = bf16[2176,256]{1,0:T(8,128)(2,1)} fusion(bf16[2176,2304]{1,0:T(8,128)(2,1)S(1)} %bitcast.84, bf16[2304,256]{1,0:T(8,128)(2,1)S(1)} %bitcast.79, bf16[2176,256]{1,0:T(8,128)(2,1)S(1)} %bitcast.67), kind=kOutput, calls=%fused_computation.5 | convolution fusion | flops 2568585216 | bytes 13434880 | tf_op jit(solution)/shard_map/dot_general | solution.py:92
  135.7 150.1 %all-reduce.9.cloned.1.call-done = (f32[2304,256]{1,0:T(8,128)}, f32[3,256,256]{2,1,0:T(8,128)}) async-done(((f32[2304,256]{1,0:T(8,128)}, f32[3,256,256]{2,1,0:T(8,128)}), (f32[2304,256]{1,0:T(8,128)}, f32[3,256,256]{2,1,0:T(8,128)})) %all-reduce.9.cloned.1.call-update) | async-done | bytes 3145744 | tf_op jit(solution)/shard_map/psum | solution.py:105
  285.8 3.3 %broadcast_multiply_fusion = f32[2304,256]{1,0:T(8,128)} fusion(f32[2304,256]{1,0:T(8,128)} %get-tuple-element.4), kind=kLoop, calls=%fused_computation.31 | loop fusion | flops 589824 | bytes 4718592 | tf_op jit(solution)/shard_map/mul | solution.py:110
  289.2 0.9 broadcast_multiply_fusion.1
  (28 shorter events, 0.3 us)
Async XLA Ops:
  7.2 6.3 %copy-start.9 = (bf16[3,256,256]{2,1,0:T(8,128)(2,1)S(1)}, bf16[3,256,256]{2,1,0:T(8,128)(2,1)}, u32[]{:S(2)}) copy-start(bf16[3,256,256]{2,1,0:T(8,128)(2,1)} %param.7) | copy-start | bytes 1179652
  7.2 6.3 %copy-start = (bf16[1,17,2,64,256]{4,3,2,1,0:T(8,128)(2,1)S(1)}, bf16[1,17,2,64,256]{4,3,2,1,0:T(8,128)(2,1)}, u32[]{:S(2)}) copy-start(bf16[1,17,2,64,256]{4,3,2,1,0:T(8,128)(2,1)} %param.5) | copy-start | bytes 3342340
  7.2 113.7 %all-reduce.11.cloned.1.call-start = ((), (), s32[]{:S(2)}) async-start(), calls=%async_computation.1 | async-start | bytes 6291456 | tf_op jit(solution)/shard_map/psum | solution.py:105
  8.6 15.4 %collective-permute-start = (bf16[1,17,1,64,256]{4,3,2,1,0:T(8,128)(2,1)S(1)}, bf16[1,17,1,64,256]{4,3,2,1,0:T(8,128)(2,1)S(1)}, u32[]{:S(2)}, u32[]{:S(2)}) collective-permute-start(bf16[1,17,1,64,256]{4,3,2,1,0:T(8,128)(2,1)S(1)} %get-tuple-element.14), channel_id=1, source_target_pairs={{0,1},{1,2},{2,3},{3,4},{4,5},{5,6},{6,7},{7,8},{8,9},{9,10},{10,1... | collective-permute-start | bytes 1671176 | tf_op jit(solution)/shard_map/ppermute | solution.py:16
  12.2 16.0 %collective-permute-start.1 = (bf16[1,17,1,64,256]{4,3,2,1,0:T(8,128)(2,1)S(1)}, bf16[1,17,1,64,256]{4,3,2,1,0:T(8,128)(2,1)S(1)}, u32[]{:S(2)}, u32[]{:S(2)}) collective-permute-start(bf16[1,17,1,64,256]{4,3,2,1,0:T(8,128)(2,1)S(1)} %get-tuple-element.15), channel_id=1, source_target_pairs={{1,0},{2,1},{3,2},{4,3},{5,4},{6,5},{7,6},{8,7},{9,8},{10,9},{11,1... | collective-permute-start | bytes 1671176 | tf_op jit(solution)/shard_map/ppermute | solution.py:18
  14.2 14.0 %copy-start.1 = (bf16[1,17,2,64,256]{4,3,2,1,0:T(8,128)(2,1)S(1)}, bf16[1,17,2,64,256]{4,3,2,1,0:T(8,128)(2,1)}, u32[]{:S(2)}) copy-start(bf16[1,17,2,64,256]{4,3,2,1,0:T(8,128)(2,1)} %param.4) | copy-start | bytes 3342340
  31.7 1.3 copy-start.7
  35.8 6.0 %copy-start.3 = (bf16[2176,256]{1,0:T(8,128)(2,1)}, bf16[2176,256]{1,0:T(8,128)(2,1)S(1)}, u32[]{:S(2)}) copy-start(bf16[2176,256]{1,0:T(8,128)(2,1)S(1)} %get-tuple-element.16) | copy-start | bytes 3342340
  36.9 4.4 %copy-start.5 = (bf16[2176,256]{1,0:T(8,128)(2,1)}, bf16[2176,256]{1,0:T(8,128)(2,1)S(1)}, u32[]{:S(2)}) copy-start(bf16[2176,256]{1,0:T(8,128)(2,1)S(1)} %fusion.9) | copy-start | bytes 3342340
  42.1 1.0 copy-start.2
  44.2 241.7 %all-reduce.9.cloned.1.call-start = ((), (), s32[]{:S(2)}) async-start(), calls=%async_computation | async-start | bytes 6291456 | tf_op jit(solution)/shard_map/psum | solution.py:105
  46.6 8.1 %copy-start.4 = (bf16[2176,256]{1,0:T(8,128)(2,1)S(1)}, bf16[2176,256]{1,0:T(8,128)(2,1)}, u32[]{:S(2)}) copy-start(bf16[2176,256]{1,0:T(8,128)(2,1)} %copy-done.3) | copy-start | bytes 3342340
  49.1 76.8 %collective-permute-start.2 = (bf16[1,17,1,64,256]{4,3,2,1,0:T(8,128)(2,1)}, bf16[1,17,1,64,256]{4,3,2,1,0:T(8,128)(2,1)}, u32[]{:S(2)}, u32[]{:S(2)}) collective-permute-start(bf16[1,17,1,64,256]{4,3,2,1,0:T(8,128)(2,1)} %get-tuple-element.8), channel_id=1, source_target_pairs={{0,1},{1,2},{2,3},{3,4},{4,5},{5,6},{6,7},{7,8},{8,9},{9,10},{10,1... | collective-permute-start | bytes 1671176 | tf_op jit(solution)/shard_map/ppermute | solution.py:16
  53.4 72.5 %collective-permute-start.3 = (bf16[1,17,1,64,256]{4,3,2,1,0:T(8,128)(2,1)}, bf16[1,17,1,64,256]{4,3,2,1,0:T(8,128)(2,1)}, u32[]{:S(2)}, u32[]{:S(2)}) collective-permute-start(bf16[1,17,1,64,256]{4,3,2,1,0:T(8,128)(2,1)} %get-tuple-element.9), channel_id=1, source_target_pairs={{1,0},{2,1},{3,2},{4,3},{5,4},{6,5},{7,6},{8,7},{9,8},{10,9},{11,1... | collective-permute-start | bytes 1671176 | tf_op jit(solution)/shard_map/ppermute | solution.py:18
  123.4 2.5 copy-start.6
  130.7 1.3 copy-start.8
  285.8 3.4 %copy-start.10 = (f32[3,256,256]{2,1,0:T(8,128)S(1)}, f32[3,256,256]{2,1,0:T(8,128)}, u32[]{:S(2)}) copy-start(f32[3,256,256]{2,1,0:T(8,128)} %get-tuple-element.5) | copy-start | bytes 2359300
Sparse Core Ops, SparseCore 0:
  44.3 76.5 all-reduce.10
  124.5 161.2 all-reduce.8
